TPU v7x, 256 devices: a whole 4x4x8 slice. The times are simulated.
256 devices in a mesh: member: 8 (over y, z_hi), tile: 32 (over z_lo, x, core).
Axes of the slice: x: 4, y: 4, z: 8 (z_hi: 2, z_lo: 4; z = z_hi * 4 + z_lo), core: 2. Of those that a mesh axis runs over, the one named last changes fastest.
Arguments:
- surface: float32 [16, 1024, 512], P('member', 'tile'), may hold values from -6 to 6
- depth: float32 [1024, 512], P('tile'), may hold values from 0.32 to 0.45
- land: int32 [1024, 512], P('tile'), may hold values from 0 to 1, as said below
- gauge_cells: int32 [400], replicated, may hold values from 0 to 524287, as said below
- sigma: float32 [400], replicated, may hold values from 0.2 to 1
- observed: float32 [9600], replicated, may hold values from -4 to 4
- noise: float32 [16, 9600], P('member'), may hold values from -3 to 3
Outputs:
- updated: float32 [16, 1024, 512], P('member', 'tile')
- records: float32 [16, 9600], P('member', 'tile')
Inputs may be any that keep to these rules, and one draw needn't show every extreme that they name: `gauge_cells`: every block of 32 rows starting at a multiple of 32 holds a gauge in its first row and one in its last row. `land`: every gauge cell and the cells directly above and below it (rows taken periodically) are sea.
All inputs are finite; a program needn't handle non-finite values.
Results may differ from a plain program's by a relative error of at most 0.00022.
Values sent between devices are 32-bit elements; how exact they have to be, the bound alone decides.
A program may use at most 64 MiB of HBM per device.

v0:
```python
import jax
import jax.numpy as jnp
from jax import lax
from jax.sharding import PartitionSpec as P

STEPS = 24


def shifted(value, axis, steps):
    count = lax.axis_size(axis)
    pairs = [(source, (source + steps) % count) for source in range(count)]
    return lax.ppermute(value, axis, pairs)


def chol_solve(factor, rhs):
    middle = lax.linalg.triangular_solve(factor, rhs, left_side=True, lower=True, transpose_a=False)
    return lax.linalg.triangular_solve(factor, middle, left_side=True, lower=True, transpose_a=True)


def member_grams(gathered, weight):
    all_records, all_innovation = gathered
    anomaly = all_records - jnp.mean(all_records, axis=0, keepdims=True)
    weighted = anomaly * weight[None, :]
    gram_ss = jnp.dot(weighted, anomaly.T, precision=lax.Precision.HIGHEST)
    gram_se = jnp.dot(weighted, all_innovation.T, precision=lax.Precision.HIGHEST)
    return (gram_ss, gram_se)


def shards(surface, depth, land, gauge_cells, sigma, observed, noise):
    member_dev, row_count, col_count = surface.shape
    tile_count = lax.axis_size("tile")
    member_total = member_dev * lax.axis_size("member")
    wet_depth = depth * land.astype(jnp.float32)
    cell_count = row_count * col_count
    local_cell = gauge_cells - lax.axis_index("tile") * cell_count
    gauge_here = ((local_cell >= 0) & (local_cell < cell_count)).astype(jnp.float32)
    gauge_pos = jnp.clip(local_cell, 0, cell_count - 1)
    next_first = shifted(wet_depth[0:1], "tile", -1)
    zero_col = jnp.zeros((row_count, 1), jnp.float32)
    coeff_rows = jnp.minimum(wet_depth, jnp.concatenate([wet_depth[1:], next_first], 0))
    coeff_cols = jnp.minimum(wet_depth, jnp.concatenate([wet_depth[:, 1:], zero_col], 1))

    def advance(carry, ignored):
        level, flux_rows, flux_cols = carry
        next_row = shifted(level[:, 0:1, :], "tile", -1)
        member_rows = level.shape[0]
        below = jnp.concatenate([level[:, 1:], next_row], 1)
        flux_rows = flux_rows - coeff_rows * (below - level)
        level_col = jnp.zeros((member_rows, row_count, 1), jnp.float32)
        beside = jnp.concatenate([level[:, :, 1:], level_col], 2)
        flux_cols = flux_cols - coeff_cols * (beside - level)
        prior_row = shifted(flux_rows[:, -1:, :], "tile", 1)
        above = jnp.concatenate([prior_row, flux_rows[:, :-1]], 1)
        left = jnp.concatenate([level_col, flux_cols[:, :, :-1]], 2)
        level = level - (flux_rows - above + flux_cols - left)
        sample = jnp.take(level.reshape(member_dev, -1), gauge_pos, axis=1) * gauge_here[None, :]
        return ((level, flux_rows, flux_cols), sample)

    start = (surface, jnp.zeros_like(surface), jnp.zeros_like(surface))
    final, samples = lax.scan(advance, start, None, length=STEPS)
    partial_records = jnp.transpose(samples, (1, 0, 2)).reshape(member_dev, -1)
    data_count = partial_records.shape[1]
    piece_count = data_count // tile_count
    piece_start = lax.axis_index("tile") * piece_count
    weight = jnp.tile(1.0 / (sigma * sigma), data_count // sigma.shape[0])
    summed = lax.psum(partial_records, "tile")
    innovation = observed[None, :] + noise - summed
    gathered = (
        lax.all_gather(summed, "member", axis=0, tiled=True),
        lax.all_gather(innovation, "member", axis=0, tiled=True),
    )
    gram_ss, gram_se = member_grams(gathered, weight)
    out_records = lax.dynamic_slice_in_dim(summed, piece_start, piece_count, 1)
    identity = jnp.eye(member_total, dtype=jnp.float32)
    system = gram_ss + (member_total - 1.0) * identity
    factor = jnp.linalg.cholesky(system)
    mixing = chol_solve(factor, gram_se)
    combine = identity + mixing - jnp.mean(mixing, axis=0, keepdims=True)
    first_member = lax.axis_index("member") * member_dev
    local_combine = lax.dynamic_slice_in_dim(combine, first_member, member_dev, 1)
    updated = jnp.einsum(
        "kxy,km->mxy",
        lax.all_gather(surface, "member", axis=0, tiled=True),
        local_combine,
        precision=lax.Precision.HIGHEST,
    )
    return (updated, out_records)


def solution(mesh):
    in_specs = (
        P("member", "tile", None),
        P("tile", None),
        P("tile", None),
        P(),
        P(),
        P(),
        P("member", None),
    )
    out_specs = (P("member", "tile", None), P("member", "tile"))
    return jax.shard_map(shards, mesh=mesh, in_specs=in_specs, out_specs=out_specs, check_vma=False)
```

profile of v0, /device:TPU:1, one launch (start us, length us, event | category | flops | bytes accessed | tf_op | source)
XLA Modules:
  0.0 833.4 jit_solution(1827644809511835850)
XLA Ops:
  14.6 449.6 %while.17 = (s32[]{:T(128)}, f32[2,32,512]{2,1,0:T(8,128)S(1)}, f32[2,32,512]{2,1,0:T(8,128)S(1)}, f32[2,32,512]{2,1,0:T(8,128)S(1)}, f32[24,2,400]{1,2,0:T(8,12...) while((s32[]{:T(128)}, f32[2,32,512]{2,1,0:T(8,128)S(1)}, ...), condition=%wide.region_1.2_spmd.clone, body=%wide.region_0.1_spmd.clone.sunk | while | flops 464979 | bytes 2890483 | solution.py:60
  36.1 6.3 collective-permute-start
  54.8 6.3 collective-permute-start
  73.4 6.3 collective-permute-start
  92.0 6.3 collective-permute-start
  110.6 6.3 collective-permute-start
  129.2 6.3 collective-permute-start
  147.8 6.3 collective-permute-start
  166.4 6.3 collective-permute-start
  185.0 6.3 collective-permute-start
  203.6 6.3 collective-permute-start
  222.3 6.3 collective-permute-start
  240.9 6.3 collective-permute-start
  259.5 6.3 collective-permute-start
  278.1 6.3 collective-permute-start
  296.7 6.3 collective-permute-start
  315.3 6.3 collective-permute-start
  333.9 6.3 collective-permute-start
  352.5 6.3 collective-permute-start
  371.1 6.3 collective-permute-start
  389.7 6.3 collective-permute-start
  468.8 258.7 %all-reduce.5.cloned.1.call-done = f32[2,9600]{1,0:T(2,128)} async-done(((f32[2,9600]{1,0:T(2,128)}), f32[2,9600]{1,0:T(2,128)}) %all-reduce.5.cloned.1.call-update) | async-done | bytes 76816 | tf_op jit(solution)/shard_map/psum | solution.py:66
  727.4 41.6 %all-gather = f32[8,2,9600]{2,1,0:T(2,128)S(1)} all-gather(f32[1,2,9600]{2,1,0:T(2,128)} %bitcast.56), channel_id=1, replica_groups=mesh['member'=8,'tile'=32] {'member'}, dimensions={0}, use_global_device_ids=true | all-gather | bytes 691200 | tf_op jit(solution)/shard_map/all_gather | solution.py:69
  775.7 43.8 %all-gather.1 = f32[8,2,9600]{2,1,0:T(2,128)S(1)} all-gather(f32[1,2,9600]{2,1,0:T(2,128)S(1)} %subtract_bitcast_fusion), channel_id=1, replica_groups=mesh['member'=8,'tile'=32] {'member'}, dimensions={0}, use_global_device_ids=true | all-gather | bytes 691200 | tf_op jit(solution)/shard_map/all_gather | solution.py:70
  (416 shorter events, 346.6 us)
Async XLA Ops:
  8.0 719.4 %all-reduce.5.cloned.1.call-start = ((), (), s32[]{:S(2)}) async-start(), calls=%async_computation | async-start | bytes 153600 | tf_op jit(solution)/shard_map/psum | solution.py:66
  36.1 7.1 collective-permute-start
  54.8 7.1 collective-permute-start
  73.4 7.1 collective-permute-start
  92.0 7.1 collective-permute-start
  110.6 7.1 collective-permute-start
  129.2 7.1 collective-permute-start
  147.8 7.1 collective-permute-start
  166.4 7.1 collective-permute-start
  185.0 7.1 collective-permute-start
  203.6 7.1 collective-permute-start
  222.3 7.1 collective-permute-start
  240.9 7.1 collective-permute-start
  259.5 7.1 collective-permute-start
  278.1 7.1 collective-permute-start
  296.7 7.1 collective-permute-start
  315.3 7.1 collective-permute-start
  333.9 7.1 collective-permute-start
  352.5 7.1 collective-permute-start
  371.1 7.1 collective-permute-start
  389.7 7.1 collective-permute-start
  408.3 7.1 collective-permute-start
  426.9 7.1 collective-permute-start
  468.0 354.8 %all-gather.4.cloned.1.call-start = ((), (), s32[]{:S(2)}) async-start(), calls=%async_computation.1 | async-start | bytes 1179648 | tf_op jit(solution)/shard_map/all_gather | solution.py:83
  (30 other events, 673.1 us)
Sparse Core Ops, SparseCore 0:
  468.1 259.2 all-reduce.4
Sparse Core Ops, SparseCore 1:
  471.1 61.8 all-gather.3
where the time goes:
time: 846 us; the launch traced here: 833 us
  waiting for transfers between devices  308 us (36%)
  local copies, waits for them, and re-layouts  230 us (27%)
  starting transfers between devices  154 us (18%)
  blocking collectives  85.4 us (10%)
  other arithmetic  34.2 us (4%)
  between operations  15.6 us (2%)
    psum x1, waiting for transfers between devices, shards(): summed = lax.psum(partial_records, 'tile')  259 us
    ppermute x49, starting transfers between devices, shifted(): return lax.ppermute(value, axis, pairs)  154 us
    sub x24, local copies, waits for them, and re-layouts, advance(): level = level - (flux_rows - above + flux_cols - left)  111 us
    gather x24, local copies, waits for them, and re-layouts, advance(): jnp.take(level.reshape(member_dev, -1), gauge_pos, axis=1)  108 us
    ppermute x49, waiting for transfers between devices, shifted(): return lax.ppermute(value, axis, pairs)  48.4 us
    all_gather x1, blocking collectives, shards(): lax.all_gather(innovation, 'member', axis=0, tiled=True)  43.8 us
    all_gather x1, blocking collectives, shards(): lax.all_gather(summed, 'member', axis=0, tiled=True)  41.6 us
    dynamic_update_slice x24, other arithmetic, shards(): final, samples = lax.scan(advance, start, None, length=STEPS)  20.8 us
  transfers between devices with their start and end apart: 51, of which 49 were waited for; matrix products, arithmetic and copies ran while one was open for 2% of the time, Pallas kernels for 0%

commit v1 on v0

v1 whole, which is shorter than its diff:
```python
import functools

import jax
import jax.numpy as jnp
from jax import lax
from jax.experimental import pallas as pl
from jax.experimental.pallas import tpu as pltpu
from jax.sharding import PartitionSpec as P

MESH = pl.DeviceIdType.MESH
STEPS = 24
HALO = 24
OWN = 32
ROWS = 96
COLT = 4
PLANE = 8
PLANES = 4
MEMBER_DEV = 8


def remote(src, dst, send, recv, member=None, tile=None):
    device = {}
    if member is not None:
        device["member"] = member
    if tile is not None:
        device["tile"] = tile
    return pltpu.make_async_remote_copy(
        src_ref=src, dst_ref=dst, send_sem=send, recv_sem=recv, device_id=device, device_id_type=MESH
    )


def next_col(value, lane, axis):
    rolled = pltpu.roll(value, 127, value.ndim - 1)
    first = lax.slice_in_dim(rolled, 0, 1, axis=axis)
    rest = lax.slice_in_dim(rolled, 1, COLT, axis=axis)
    return jnp.where(lane == 127, jnp.concatenate([rest, first], axis), rolled)


def prev_col(value, lane, axis):
    rolled = pltpu.roll(value, 1, value.ndim - 1)
    last = lax.slice_in_dim(rolled, COLT - 1, COLT, axis=axis)
    rest = lax.slice_in_dim(rolled, 0, COLT - 1, axis=axis)
    return jnp.where(lane == 0, jnp.concatenate([last, rest], axis), rolled)


def window(ref, start, lane):
    tiles = ref.shape[1] // 128
    tile = start // 128
    shift = start % 128
    after = jnp.minimum(tile + 1, tiles - 1)
    low = ref[:, pl.ds(pl.multiple_of(tile * 128, 128), 128)]
    high = ref[:, pl.ds(pl.multiple_of(after * 128, 128), 128)]
    both = jnp.where(lane < 128 - shift, pltpu.roll(low, 128 - shift, 1), pltpu.roll(high, 128 - shift, 1))
    return jnp.where(lane < 100, both, 0.0)


def kernel(
    surface, depth, land, cells, sigma, observed, noise, updated, records,
    state, frow, fcol, crow, ccol, hist, every, pieces, got1, mine, got2, own_noise, all_noise, obs, weight,
    plane_got, gram, gram1, gram_plane, gram2, coef,
    local_sem, halo_send, halo_recv, noise_send, noise_recv, s1_send, s1_recv, s2_send, s2_recv,
    zl_send, zl_recv, g1_send, g1_recv, g2_send, g2_recv, sur_send, sur_recv,
):
    a = lax.axis_index("member")
    t = lax.axis_index("tile")
    z = t // PLANE
    c = t % PLANE
    y = a // 2
    hi = a % 2
    tiles = PLANE * PLANES
    partner = a + 1 - 2 * hi
    y_next = ((y + 1) % 4) * 2
    y_prev = ((y + 3) % 4) * 2

    barrier = pltpu.get_barrier_semaphore()

    def greet(**device):
        pl.semaphore_signal(barrier, inc=1, device_id=device, device_id_type=MESH)

    for k in range(1, MEMBER_DEV):
        greet(member=(a + k) % MEMBER_DEV)
    for k in range(1, PLANE):
        greet(tile=z * PLANE + (c + k) % PLANE)
    for k in range(1, PLANES):
        greet(tile=((z + k) % PLANES) * PLANE + c)
    greet(tile=(t + 1) % tiles)
    greet(tile=(t + tiles - 1) % tiles)

    loads = [
        pltpu.make_async_copy(
            surface.at[:, :, pl.ds(i * 128, 128)], state.at[pl.ds(0, 2), i, pl.ds(OWN, 32), :], local_sem.at[i]
        )
        for i in range(COLT)
    ]
    for load in loads:
        load.start()
    keep = pltpu.make_async_copy(surface, every.at[a], local_sem.at[COLT])
    keep.start()

    for i in range(COLT):
        columns = slice(i * 128, (i + 1) * 128)
        state[2, i, OWN:OWN + 32, :] = depth[:, columns] * land[:, columns].astype(jnp.float32)
    state[:, :, 0:8, :] = jnp.zeros((3, COLT, 8, 128), jnp.float32)
    state[:, :, ROWS - 8:ROWS, :] = jnp.zeros((3, COLT, 8, 128), jnp.float32)
    for r in range(0, ROWS, 8):
        frow[:, :, r:r + 8, :] = jnp.zeros((2, COLT, 8, 128), jnp.float32)
        fcol[:, :, r:r + 8, :] = jnp.zeros((2, COLT, 8, 128), jnp.float32)
    for load in loads:
        load.wait()
    pl.semaphore_wait(barrier, MEMBER_DEV - 1 + PLANE - 1 + PLANES - 1 + 2)

    up = remote(
        state.at[:, :, pl.ds(OWN, HALO), :], state.at[:, :, pl.ds(OWN + 32, HALO), :],
        halo_send.at[0], halo_recv.at[0], tile=(t + tiles - 1) % tiles,
    )
    down = remote(
        state.at[:, :, pl.ds(OWN + 32 - HALO, HALO), :], state.at[:, :, pl.ds(OWN - HALO, HALO), :],
        halo_send.at[1], halo_recv.at[1], tile=(t + 1) % tiles,
    )
    up.start()
    down.start()

    def block(number, slot, member, part=None):
        ref = every.at[slot] if part is None else every.at[slot, part]
        return remote(ref, ref, sur_send.at[number], sur_recv.at[number], member=member)

    keep.wait()
    to_partner = block(0, a, partner)
    to_next = block(1, a, y_next + hi)
    to_prev = block(2, a, y_prev + hi)
    to_partner.start()
    to_next.start()
    to_prev.start()

    lane1 = lax.broadcasted_iota(jnp.int32, (1, 128), 1)
    lane2 = lax.broadcasted_iota(jnp.int32, (2, 128), 1)
    for p in range(PLANES):
        own_noise[p, 6:8, :] = jnp.zeros((2, 128), jnp.float32)
        for r in range(3):
            unit = (p * PLANE + c) * 3 + r
            own_noise[p, 2 * r:2 * r + 2, :] = window(noise, unit * 100, lane2)
            obs[p, r:r + 1, :] = window(observed, unit * 100, lane1)
    for q in range(4):
        weight[q:q + 1, :] = sigma[q:q + 1, :]
    all_noise[a] = own_noise[...]
    noise_copies = []
    for k in range(1, MEMBER_DEV):
        noise_copies.append(
            remote(own_noise, all_noise.at[a], noise_send.at[k], noise_recv.at[a], member=(a + k) % MEMBER_DEV)
        )
        noise_copies[-1].start()

    up.wait()
    down.wait()

    lane3 = lax.broadcasted_iota(jnp.int32, (COLT, 8, 128), 2)
    tile3 = lax.broadcasted_iota(jnp.int32, (COLT, 8, 128), 0)
    for r in range(8, ROWS - 8, 8):
        wet = state[2, :, r:r + 8, :]
        crow[:, r:r + 8, :] = jnp.minimum(wet, state[2, :, r + 1:r + 9, :])
        beside = jnp.where((lane3 == 127) & (tile3 == COLT - 1), 0.0, next_col(wet, lane3, 0))
        ccol[:, r:r + 8, :] = jnp.minimum(wet, beside)

    lane4 = lax.broadcasted_iota(jnp.int32, (2, COLT, 8, 128), 3)

    def advance(first, last, s):
        for b in range(first, last):
            r = 8 + 8 * b
            level = state[0:2, :, r:r + 8, :]
            below = state[0:2, :, r + 1:r + 9, :]
            rows_flux = frow[:, :, r:r + 8, :] - crow[:, r:r + 8, :][None] * (below - level)
            frow[:, :, r:r + 8, :] = rows_flux
            beside = next_col(level, lane4, 1)
            cols_flux = fcol[:, :, r:r + 8, :] - ccol[:, r:r + 8, :][None] * (beside - level)
            fcol[:, :, r:r + 8, :] = cols_flux
            above = frow[:, :, r - 1:r + 7, :]
            left = prev_col(cols_flux, lane4, 1)
            level = level - (rows_flux - above + cols_flux - left)
            state[0:2, :, r:r + 8, :] = level
            if 3 <= b < 7:
                for m in range(2):
                    for i in range(COLT):
                        hist[pl.ds(i * 32 + 8 * (b - 3), 8), 2 * s + m, :] = level[m, i]

    for phase in range(3):
        def one(s, carry, phase=phase):
            advance(phase, 10 - phase, s)
            return carry

        lax.fori_loop(8 * phase, 8 * phase + 8, one, 0)

    lane48 = lax.broadcasted_iota(jnp.int32, (2 * STEPS, 128), 1)
    base = t * (32 * 512)

    def sample(j, totals):
        out = []
        for q in range(4):
            local = cells[q * 100 + j] - base
            here = (local >= 0) & (local < 32 * 512)
            cell = jnp.clip(local, 0, 32 * 512 - 1)
            col = cell % 512
            found = hist[(col // 128) * 32 + cell // 512]
            moved = pltpu.roll(found, (j - col % 128 + 128) % 128, 1)
            lane_here = jnp.where(here, j, -1)
            out.append(jnp.where(lane48 == lane_here, moved, totals[q]))
        return tuple(out)

    zero48 = jnp.zeros((2 * STEPS, 128), jnp.float32)
    totals = lax.fori_loop(0, 100, sample, (zero48,) * 4)
    for p in range(PLANES):
        for k in range(PLANE):
            pieces[k, p, 6:8, :] = jnp.zeros((2, 128), jnp.float32)
            for r in range(3):
                unit = (p * PLANE + k) * 3 + r
                s, q = unit // 4, unit % 4
                pieces[k, p, 2 * r:2 * r + 2, :] = totals[q][2 * s:2 * s + 2, :]

    copies1 = []
    for k in range(1, PLANE):
        other = (c + k) % PLANE
        copies1.append(
            remote(pieces.at[other], got1.at[c], s1_send.at[k], s1_recv.at[c], tile=z * PLANE + other)
        )
        copies1[-1].start()
    total = pieces[c]
    for k in range(1, PLANE):
        other = (c + k) % PLANE
        remote(pieces.at[other], got1.at[other], s1_send.at[k], s1_recv.at[other], tile=z * PLANE + other).wait_recv()
        total = total + got1[other]
    mine[...] = total
    got2[a] = total

    copies2 = []
    for k in range(1, MEMBER_DEV):
        other = (a + k) % MEMBER_DEV
        copies2.append(remote(mine, got2.at[a], s2_send.at[k], s2_recv.at[a], member=other))
        copies2[-1].start()
    copies_z = []
    for k in range(1, PLANES):
        other = (z + k) % PLANES
        copies_z.append(
            remote(mine.at[other], plane_got.at[z], zl_send.at[k], zl_recv.at[z], tile=other * PLANE + c)
        )
        copies_z[-1].start()

    to_next.wait()
    to_prev.wait()
    on_next = block(3, y_prev + hi, y_next + hi, 0)
    on_prev = block(4, y_next + hi, y_prev + hi, 1)
    on_next.start()
    on_prev.start()

    for k in range(1, MEMBER_DEV):
        other = (a + k) % MEMBER_DEV
        remote(own_noise, all_noise.at[other], noise_send.at[k], noise_recv.at[other], member=other).wait_recv()
    for k in range(1, MEMBER_DEV):
        other = (a + k) % MEMBER_DEV
        remote(mine, got2.at[other], s2_send.at[k], s2_recv.at[other], member=other).wait_recv()

    lefts, rights = [], []
    for p in range(PLANES):
        for r in range(3):
            group = ((p * PLANE + c) * 3 + r) % 4
            sig = weight[pl.ds(group, 1), :]
            wgt = jnp.where(lane1 < 100, 1.0 / (sig * sig), 0.0)
            rec = got2[:, p, 2 * r:2 * r + 2, :].reshape(16, 128)
            nse = all_noise[:, p, 2 * r:2 * r + 2, :].reshape(16, 128)
            innovation = obs[p, r:r + 1, :] + nse - rec
            anomaly = rec - jnp.sum(rec, axis=0, keepdims=True) * (1.0 / 16.0)
            lefts.append(anomaly * wgt)
            rights.append(jnp.concatenate([anomaly, innovation], 0))
    left = jnp.concatenate(lefts, 1)
    right = jnp.concatenate(rights, 1)
    both = lax.dot_general(
        left, right, (((1,), (1,)), ((), ())), precision=lax.Precision.HIGHEST, preferred_element_type=jnp.float32
    )
    gram[:, 0:32] = both

    def exchange(count, me, src, dst, send, recv, tile_of):
        sent = []
        for k in range(1, count):
            other = (me + k) % count
            sent.append(remote(src, dst.at[me], send.at[k], recv.at[me], tile=tile_of(other)))
            sent[-1].start()
        return sent

    def collect(count, me, src, dst, send, recv, tile_of):
        total = None
        for k in range(1, count):
            other = (me + k) % count
            remote(src, dst.at[other], send.at[k], recv.at[other], tile=tile_of(other)).wait_recv()
        for k in range(count):
            total = dst[k] if total is None else total + dst[k]
        return total

    def in_plane(other):
        return z * PLANE + other

    def across(other):
        return other * PLANE + c

    gram1[c] = gram[...]
    sent1 = exchange(PLANE, c, gram, gram1, g1_send, g1_recv, in_plane)

    to_partner.wait()
    par_next = block(5, partner, y_next + hi)
    par_prev = block(6, partner, y_prev + hi)
    par_next.start()
    par_prev.start()

    plane_total = collect(PLANE, c, gram, gram1, g1_send, g1_recv, in_plane)
    gram_plane[...] = plane_total
    gram2[z] = plane_total
    sent2 = exchange(PLANES, z, gram_plane, gram2, g2_send, g2_recv, across)

    block_rows = mine[z]
    for k in range(1, PLANES):
        other = (z + k) % PLANES
        remote(mine.at[other], plane_got.at[other], zl_send.at[k], zl_recv.at[other], tile=other * PLANE + c).wait_recv()
        block_rows = block_rows + plane_got[other]
    for r in range(3):
        records[:, 100 * r:100 * r + 100] = block_rows[2 * r:2 * r + 2, 0:100]

    par_next.wait()
    par_prev.wait()
    last_next = block(7, y_prev + 1 - hi, y_next + hi, 0)
    last_prev = block(8, y_next + 1 - hi, y_prev + hi, 1)
    last_next.start()
    last_prev.start()

    system = collect(PLANES, z, gram_plane, gram2, g2_send, g2_recv, across)

    lane16 = lax.broadcasted_iota(jnp.int32, (16, 128), 1)
    row16 = lax.broadcasted_iota(jnp.int32, (16, 128), 0)
    system = jnp.where(lane16 < 32, system, 0.0) + jnp.where(row16 == lane16, 15.0, 0.0)
    for p in range(16):
        pivot = system[p:p + 1, :] / system[p:p + 1, p:p + 1]
        system = jnp.where(row16 == p, pivot, system - system[:, p:p + 1] * pivot)
    combine = system - jnp.sum(system, axis=0, keepdims=True) * (1.0 / 16.0)
    combine = combine + jnp.where(row16 == lane16 - 16, 1.0, 0.0)
    for m in range(2):
        column = jnp.sum(jnp.where(lane16 == 16 + 2 * a + m, combine, 0.0), axis=1, keepdims=True)
        coef[m] = jnp.broadcast_to(column, (16, 128))

    on_next.wait()
    on_prev.wait()
    last_next.wait()
    last_prev.wait()

    factors = [[jnp.broadcast_to(coef[m, k:k + 1, :], (8, 128)) for k in range(16)] for m in range(2)]
    for r in range(0, 32, 8):
        for i in range(COLT):
            columns = slice(i * 128, (i + 1) * 128)
            sums = [None, None]
            for k in range(16):
                value = every[k // 2, k % 2, r:r + 8, columns]
                for m in range(2):
                    term = value * factors[m][k]
                    sums[m] = term if sums[m] is None else sums[m] + term
            for m in range(2):
                updated[m, r:r + 8, columns] = sums[m]

    for copy in noise_copies + copies1 + copies2 + copies_z + sent1 + sent2:
        copy.wait_send()


def shards(surface, depth, land, gauge_cells, sigma, observed, noise):
    f32 = jnp.float32
    groups = jnp.pad(sigma.reshape(4, 100), ((0, 0), (0, 28)), constant_values=1.0)
    vmem = pl.BlockSpec(memory_space=pltpu.VMEM)
    dma = pltpu.SemaphoreType.DMA
    return pl.pallas_call(
        kernel,
        out_shape=(jax.ShapeDtypeStruct((2, 32, 512), f32), jax.ShapeDtypeStruct((2, 300), f32)),
        in_specs=[
            pl.BlockSpec(memory_space=pl.ANY), vmem, vmem, pl.BlockSpec(memory_space=pltpu.SMEM), vmem, vmem, vmem,
        ],
        out_specs=(vmem, vmem),
        scratch_shapes=[
            pltpu.VMEM((3, COLT, ROWS, 128), f32),
            pltpu.VMEM((2, COLT, ROWS, 128), f32),
            pltpu.VMEM((2, COLT, ROWS, 128), f32),
            pltpu.VMEM((COLT, ROWS, 128), f32),
            pltpu.VMEM((COLT, ROWS, 128), f32),
            pltpu.VMEM((128, 2 * STEPS, 128), f32),
            pltpu.VMEM((MEMBER_DEV, 2, 32, 512), f32),
            pltpu.VMEM((PLANE, PLANES, 8, 128), f32),
            pltpu.VMEM((PLANE, PLANES, 8, 128), f32),
            pltpu.VMEM((PLANES, 8, 128), f32),
            pltpu.VMEM((MEMBER_DEV, PLANES, 8, 128), f32),
            pltpu.VMEM((PLANES, 8, 128), f32),
            pltpu.VMEM((MEMBER_DEV, PLANES, 8, 128), f32),
            pltpu.VMEM((PLANES, 8, 128), f32),
            pltpu.VMEM((8, 128), f32),
            pltpu.VMEM((PLANES, 8, 128), f32),
            pltpu.VMEM((16, 128), f32),
            pltpu.VMEM((PLANE, 16, 128), f32),
            pltpu.VMEM((16, 128), f32),
            pltpu.VMEM((PLANES, 16, 128), f32),
            pltpu.VMEM((2, 16, 128), f32),
            dma((5,)),
            dma((2,)), dma((2,)),
            dma((8,)), dma((8,)),
            dma((8,)), dma((8,)),
            dma((8,)), dma((8,)),
            dma((4,)), dma((4,)),
            dma((8,)), dma((8,)),
            dma((4,)), dma((4,)),
            dma((9,)), dma((9,)),
        ],
        compiler_params=pltpu.CompilerParams(collective_id=0, has_side_effects=True),
    )(surface, depth, land, gauge_cells, groups, observed.reshape(1, -1), noise)


def solution(mesh):
    in_specs = (
        P("member", "tile", None),
        P("tile", None),
        P("tile", None),
        P(),
        P(),
        P(),
        P("member", None),
    )
    out_specs = (P("member", "tile", None), P("member", "tile"))
    return jax.shard_map(shards, mesh=mesh, in_specs=in_specs, out_specs=out_specs, check_vma=False)
```

time: 846 us -> 67.2 us (0.08); the launches traced: 833 us -> 67 us
  waiting for transfers between devices: 308 us -> 0 us
  local copies, waits for them, and re-layouts: 230 us -> 4.92 us
  starting transfers between devices: 154 us -> 0 us
  blocking collectives: 85.4 us -> 0 us
  Pallas kernels: 0 us -> 61.4 us
  other arithmetic: 34.2 us -> 0 us
  between operations: 15.6 us -> 0.65 us
    psum x1 -> x0, waiting for transfers between devices: 259 us -> none  [shards(): summed = lax.psum(partial_records, 'tile')]
    ppermute x49 -> x0, starting transfers between devices: 154 us -> none  [shifted(): return lax.ppermute(value, axis, pairs)]
    sub x24 -> x0, local copies, waits for them, and re-layouts: 111 us -> none  [advance(): level = level - (flux_rows - above + flux_cols - left)]
    gather x24 -> x0, local copies, waits for them, and re-layouts: 108 us -> none  [advance(): jnp.take(level.reshape(member_dev, -1), gauge_pos, axis=1)]
    all_gather x2 -> x0, blocking collectives: 85.4 us -> none  [the longest x1 43.8 us: shards(): lax.all_gather(innovation, 'member', axis=0, tiled=True)]
    pallas_call x0 -> x1, Pallas kernels: none -> 61.4 us  [shards(): pl.pallas_call(kernel, out_shape=(jax.ShapeDtypeStruct((2, 32, 512), f32)...]
    ppermute x49 -> x0, waiting for transfers between devices: 48.4 us -> none  [shifted(): return lax.ppermute(value, axis, pairs)]
    dynamic_update_slice x24 -> x0, other arithmetic: 20.8 us -> none  [shards(): final, samples = lax.scan(advance, start, None, length=STEPS)]
  transfers between devices with their start and end apart: 51 -> 0, of which waited for: 49 -> 0; matrix products, arithmetic and copies ran while one was open for 2% -> 0% of each run, Pallas kernels for 0% -> 0%
where the time goes in v1:
time: 67.2 us; the launch traced here: 67 us
  Pallas kernels  61.4 us (91%)
  local copies, waits for them, and re-layouts  4.92 us (7%)
    pallas_call x1, Pallas kernels, shards(): pl.pallas_call(kernel, out_shape=(jax.ShapeDtypeStruct((2, 32, 512), f32)...  61.4 us
    unnamed x4, local copies, waits for them, and re-layouts  2.15 us
    reshape x1, local copies, waits for them, and re-layouts, shards(): observed.reshape(1, -1)  1.42 us

profile of v1, /device:TPU:1, one launch (start us, length us, event | category | flops | bytes accessed | tf_op | source)
XLA Modules:
  0.0 67.0 jit_solution(6472061165532553563)
XLA Ops:
  0.6 0.8 %reshape.10 = f32[4,100]{1,0:T(4,128)S(1)} reshape(f32[400]{0:T(512)} %param.11) | data formatting | bytes 3200 | tf_op jit(solution)/shard_map/reshape | solution.py:369
  1.4 0.6 pad.4.sigma
  2.0 1.4 %reshape.11.observed = f32[1,9600]{1,0:T(1,128)} reshape(f32[9600]{0:T(1024)} %param.12) | data formatting | bytes 76800 | tf_op jit(solution)/shard_map/reshape | solution.py:412
  3.4 61.4 %shard_map.86 = (f32[2,32,512]{2,1,0:T(8,128)}, f32[2,300]{1,0:T(2,128)}) custom-call(f32[2,32,512]{2,1,0:T(8,128)} %surface.1, f32[32,512]{1,0:T(8,128)} %depth.1, s32[32,512]{1,0:T(8,128)} %land.1, s32[400]{0:T(512)} %cells.1, f32[4,128]{1,0:T(4,128)} %pad.4.sigma, f32[1,9600]{1,0:T(1,128)} %reshape.11.observed, f32[2,9600]{1,0:T(2,128)} %noise.1), custom_call_target="tpu_custom_call" | custom-call | tf_op jit(solution)/shard_map/pallas_call | solution.py:372
  64.8 0.0 copy-start
  64.8 1.6 %copy.11 = f32[2,32,512]{2,1,0:T(8,128)} copy(f32[2,32,512]{2,1,0:T(8,128)} %get-tuple-element.4) | data formatting | bytes 262144
  66.4 0.0 copy-done
  66.4 0.6 copy.12
Async XLA Ops:
  64.8 1.6 %copy-start = (f32[2,300]{1,0:T(2,128)S(1)}, f32[2,300]{1,0:T(2,128)}, u32[]{:S(2)}) copy-start(f32[2,300]{1,0:T(2,128)} %get-tuple-element.5) | copy-start | bytes 7204

commit v2 on v1

v2 whole, which is shorter than its diff:
```python
import jax
import jax.numpy as jnp
from jax import lax
from jax.experimental import pallas as pl
from jax.experimental.pallas import tpu as pltpu
from jax.sharding import PartitionSpec as P

MESH = pl.DeviceIdType.MESH
HALO = 24
OWN = 32
ROWS = OWN + 2 * HALO
PLANE = 8
PLANES = 4
MEMBER_DEV = 8
NO_GAUGE = OWN * 32


def remote(src, dst, send, recv, **device):
    return pltpu.make_async_remote_copy(
        src_ref=src, dst_ref=dst, send_sem=send, recv_sem=recv, device_id=device, device_id_type=MESH
    )


def next_col(value, lane):
    rolled = pltpu.roll(value, 127, value.ndim - 1)
    return jnp.where(lane == 127, pltpu.roll(rolled, 7, value.ndim - 2), rolled)


def prev_col(value, lane):
    rolled = pltpu.roll(value, 1, value.ndim - 1)
    return jnp.where(lane == 0, pltpu.roll(rolled, 1, value.ndim - 2), rolled)


def merge(low, high, shift, lane):
    both = jnp.where(lane < 128 - shift, pltpu.roll(low, 128 - shift, 1), pltpu.roll(high, 128 - shift, 1))
    return jnp.where(lane < 100, both, 0.0)


def kernel(
    surface, depth, land, cells_in, sigma_in, observed_in, noise_in, updated, records,
    depth_v, land_v, cells, sigma, observed, noise, starts, shifts,
    lev, wet, frow, fcol, crow, ccol, hist, every, pieces, got1, mine, got2, own_noise, all_noise, obs,
    plane_got, block_rows, gram, gram1, gram_plane, gram2, coef,
    local_sem, halo_send, halo_recv, noise_send, noise_recv, s1_send, s1_recv, s2_send, s2_recv,
    zl_send, zl_recv, g1_send, g1_recv, g2_send, g2_recv, sur_send, sur_recv,
):
    a = lax.axis_index("member")
    t = lax.axis_index("tile")
    z = t // PLANE
    c = t % PLANE
    y = a // 2
    hi = a % 2
    tiles = PLANE * PLANES
    partner = a + 1 - 2 * hi
    y_next = ((y + 1) % 4) * 2
    y_prev = ((y + 3) % 4) * 2
    above_tile = (t + tiles - 1) % tiles
    below_tile = (t + 1) % tiles

    barrier = pltpu.get_barrier_semaphore()

    def greet(**device):
        pl.semaphore_signal(barrier, inc=1, device_id=device, device_id_type=MESH)

    for k in range(1, MEMBER_DEV):
        greet(member=(a + k) % MEMBER_DEV)
    greet(tile=below_tile)
    greet(tile=above_tile)
    for k in range(1, PLANES):
        greet(tile=((z + k) % PLANES) * PLANE + c)
    for k in range(1, PLANE):
        greet(tile=z * PLANE + (c + k) % PLANE)

    def local(number, src, dst):
        copy = pltpu.make_async_copy(src, dst, local_sem.at[number])
        copy.start()
        return copy

    loads = [local(0, depth, depth_v), local(1, land, land_v)]
    loads += [
        local(
            2 + 4 * m + i,
            surface.at[m, :, pl.ds(i * 128, 128)],
            lev.at[pl.ds(HALO, OWN), 4 * m + i, :],
        )
        for m in range(2)
        for i in range(4)
    ]
    keep = local(10, surface, every.at[a])
    late = [local(11, noise_in, noise), local(12, observed_in, observed), local(13, sigma_in, sigma)]
    table = local(14, cells_in, cells)

    lane = lax.broadcasted_iota(jnp.int32, (8, 128), 1)
    sub = lax.broadcasted_iota(jnp.int32, (8, 128), 0)
    zero = jnp.zeros((8, 128), jnp.float32)
    for r in range(ROWS):
        frow[r] = zero
        fcol[r] = zero
    for s in range(6):
        for p in range(4):
            hist[pl.ds(((s * (OWN + 1) + OWN) * 4 + p) * 8, 8), :] = zero
    loads[0].wait()
    loads[1].wait()
    for r in range(0, OWN, 8):
        for i in range(4):
            columns = slice(i * 128, (i + 1) * 128)
            value = depth_v[r:r + 8, columns] * land_v[r:r + 8, columns].astype(jnp.float32)
            wet[pl.ds((HALO + r) * 4 + i, 8, stride=4), :] = value
    for load in loads[2:]:
        load.wait()
    pl.semaphore_wait(barrier, MEMBER_DEV - 1 + PLANE - 1 + PLANES - 1 + 2)

    halos = [
        remote(lev.at[pl.ds(HALO, HALO)], lev.at[pl.ds(HALO + OWN, HALO)], halo_send.at[0], halo_recv.at[0], tile=above_tile),
        remote(lev.at[pl.ds(OWN, HALO)], lev.at[pl.ds(0, HALO)], halo_send.at[1], halo_recv.at[1], tile=below_tile),
        remote(
            wet.at[pl.ds(HALO * 4, HALO * 4)], wet.at[pl.ds((HALO + OWN) * 4, HALO * 4)],
            halo_send.at[2], halo_recv.at[2], tile=above_tile,
        ),
        remote(
            wet.at[pl.ds(OWN * 4, HALO * 4)], wet.at[pl.ds(0, HALO * 4)],
            halo_send.at[3], halo_recv.at[3], tile=below_tile,
        ),
    ]
    for copy in halos:
        copy.start()

    def block(number, slot, member, part=None):
        ref = every.at[slot] if part is None else every.at[slot, part]
        return remote(ref, ref, sur_send.at[number], sur_recv.at[number], member=member)

    keep.wait()
    to_partner = block(0, a, partner)
    to_next = block(1, a, y_next + hi)
    to_prev = block(2, a, y_prev + hi)
    to_partner.start()
    to_next.start()
    to_prev.start()

    lane1 = lax.broadcasted_iota(jnp.int32, (1, 128), 1)
    lane2 = lax.broadcasted_iota(jnp.int32, (2, 128), 1)
    for load in late:
        load.wait()
    for p in range(PLANES):
        for r in range(3):
            start = ((p * PLANE + c) * 3 + r) * 100
            first, shift = start // 128, start % 128
            after = jnp.minimum(first + 1, 74)
            own_noise[r, 2 * p:2 * p + 2, :] = merge(
                noise[:, pl.ds(pl.multiple_of(first * 128, 128), 128)],
                noise[:, pl.ds(pl.multiple_of(after * 128, 128), 128)],
                shift, lane2,
            )
            obs[r, p:p + 1, :] = merge(observed[pl.ds(first, 1), :], observed[pl.ds(after, 1), :], shift, lane1)
    all_noise[a] = own_noise[...]
    noise_copies = []
    for k in range(1, MEMBER_DEV):
        noise_copies.append(
            remote(own_noise, all_noise.at[a], noise_send.at[k], noise_recv.at[a], member=(a + k) % MEMBER_DEV)
        )
        noise_copies[-1].start()

    table.wait()

    def entry(j, carry):
        for q in range(4):
            cell = cells[q * 100 + j]
            start = ((cell >> 9) & 31) * 32 + ((cell >> 7) & 3)
            starts[q * 100 + j] = jnp.where((cell >> 14) == t, start, NO_GAUGE)
            shifts[q * 100 + j] = (j - cell) & 127
        return carry

    lax.fori_loop(0, 100, entry, 0, unroll=5)

    edge = (lane == 127) & ((sub & 3) == 3)

    def both_rows(pair):
        value = wet[8 * pair:8 * pair + 8, :]
        other = pltpu.roll(value, 4, 0)
        return [jnp.where(sub < 4, value, other), jnp.where(sub < 4, other, value)]

    def coefficients(first, last):
        below = None
        for pair in range(last // 2 - 1, first // 2 - 1, -1):
            even, odd = both_rows(pair)
            if below is None:
                below = both_rows(last // 2)[0] if last < ROWS else zero
            for r, value, following in ((2 * pair + 1, odd, below), (2 * pair, even, odd)):
                crow[r] = jnp.minimum(value, following)
                ccol[r] = jnp.minimum(value, jnp.where(edge, 0.0, next_col(value, lane)))
            below = even

    coefficients(HALO, HALO + OWN - 2)
    for copy in halos:
        copy.wait()
    coefficients(0, HALO)
    coefficients(HALO + OWN - 2, ROWS)

    def advance(first, s):
        low, high = first + 1, ROWS - 1 - first
        level = lev[low - 1:low]
        flux = frow[low - 1:low] - crow[low - 1:low] * (lev[low:low + 1] - level)
        frow[low - 1:low] = flux
        group = (s % 6) * (OWN + 1)
        for start in range(low, high, 8):
            stop = min(start + 8, high)
            lane3 = lax.broadcasted_iota(jnp.int32, (stop - start, 8, 128), 2)
            level = lev[start:stop]
            rows_flux = frow[start:stop] - crow[start:stop] * (lev[start + 1:stop + 1] - level)
            frow[start:stop] = rows_flux
            cols_flux = fcol[start:stop] - ccol[start:stop] * (next_col(level, lane3) - level)
            fcol[start:stop] = cols_flux
            above = jnp.concatenate([flux, rows_flux[:-1]], 0)
            flux = rows_flux[-1:]
            level = level - (rows_flux - above + cols_flux - prev_col(cols_flux, lane3))
            lev[start:stop] = level
            for r in range(max(start, HALO), min(stop, HALO + OWN)):
                flat = ((group + (r - HALO)) * 4 + s // 6) * 8
                hist[pl.ds(pl.multiple_of(flat, 8), 8), :] = level[r - start]

    for first in range(0, 24, 8):
        def one(s, carry, first=first):
            advance(first, s)
            return carry

        lax.fori_loop(first, first + 8, one, 0)

    def sample(j, totals):
        put = lane == j
        out = []
        for q in range(4):
            start = starts[q * 100 + j]
            shift = shifts[q * 100 + j]
            for s in range(6):
                found = hist[pl.ds(s * (OWN + 1) * 32 + start, 8, stride=4), :]
                out.append(jnp.where(put, pltpu.roll(found, shift, 1), totals[q * 6 + s]))
        return tuple(out)

    totals = lax.fori_loop(0, 100, sample, (zero,) * 24, unroll=4)
    for q in range(4):
        for s in range(6):
            pieces[4 * s + q] = totals[q * 6 + s]

    copies1 = []
    for k in range(1, PLANE):
        other = (c + k) % PLANE
        copies1.append(
            remote(pieces.at[pl.ds(other * 3, 3)], got1.at[c], s1_send.at[k], s1_recv.at[c], tile=z * PLANE + other)
        )
        copies1[-1].start()
    total = pieces[pl.ds(c * 3, 3)]
    for k in range(1, PLANE):
        other = (c + k) % PLANE
        remote(
            pieces.at[pl.ds(other * 3, 3)], got1.at[other], s1_send.at[k], s1_recv.at[other], tile=z * PLANE + other
        ).wait_recv()
        total = total + got1[other]
    mine[...] = total
    for r in range(3):
        got2[pl.ds(pl.multiple_of(a * 24 + 8 * r, 8), 8), :] = total[r]

    def slot(ref, number):
        return ref.at[pl.ds(pl.multiple_of(number * 24, 8), 24)]

    flat_mine = got2.at[pl.ds(pl.multiple_of(a * 24, 8), 24)]
    copies2 = []
    for k in range(1, MEMBER_DEV):
        other = (a + k) % MEMBER_DEV
        copies2.append(remote(flat_mine, slot(got2, a), s2_send.at[k], s2_recv.at[a], member=other))
        copies2[-1].start()
    copies_z = []
    for k in range(1, PLANES):
        other = (z + k) % PLANES
        copies_z.append(remote(mine, plane_got.at[z], zl_send.at[k], zl_recv.at[z], tile=other * PLANE + c))
        copies_z[-1].start()

    to_next.wait()
    to_prev.wait()
    on_next = block(3, y_prev + hi, y_next + hi, 0)
    on_prev = block(4, y_next + hi, y_prev + hi, 1)
    on_next.start()
    on_prev.start()

    for k in range(1, MEMBER_DEV):
        other = (a + k) % MEMBER_DEV
        remote(own_noise, all_noise.at[other], noise_send.at[k], noise_recv.at[other], member=other).wait_recv()
    for k in range(1, MEMBER_DEV):
        other = (a + k) % MEMBER_DEV
        remote(flat_mine, slot(got2, other), s2_send.at[k], s2_recv.at[other], member=other).wait_recv()

    lefts, rights = [], []
    for p in range(PLANES):
        for r in range(3):
            group = ((p * PLANE + c) * 3 + r) % 4
            sig = sigma[pl.ds(group, 1), :]
            wgt = jnp.where(lane1 < 100, 1.0 / (sig * sig), 0.0)
            rec = jnp.concatenate(
                [got2[pl.ds(8 * r + 2 * p + m, 8, stride=24), :] for m in range(2)], 0
            )
            nse = jnp.concatenate([all_noise[:, r, 2 * p + m, :] for m in range(2)], 0)
            innovation = obs[r, p:p + 1, :] + nse - rec
            anomaly = rec - jnp.sum(rec, axis=0, keepdims=True) * (1.0 / 16.0)
            lefts.append(anomaly * wgt)
            rights.append(jnp.concatenate([anomaly, innovation], 0))
    both = lax.dot_general(
        jnp.concatenate(lefts, 1), jnp.concatenate(rights, 1), (((1,), (1,)), ((), ())),
        precision=lax.Precision.HIGHEST, preferred_element_type=jnp.float32,
    )
    gram[:, 0:64] = jnp.concatenate([both[0:8], both[8:16]], 1)
    gram[:, 64:128] = jnp.zeros((8, 64), jnp.float32)

    def exchange(count, me, src, dst, send, recv, tile_of):
        sent = []
        for k in range(1, count):
            other = (me + k) % count
            sent.append(remote(src, dst.at[me], send.at[k], recv.at[me], tile=tile_of(other)))
            sent[-1].start()
        return sent

    def collect(count, me, src, dst, send, recv, tile_of):
        for k in range(1, count):
            other = (me + k) % count
            remote(src, dst.at[other], send.at[k], recv.at[other], tile=tile_of(other)).wait_recv()
        parts = [dst[k] for k in range(count)]
        while len(parts) > 1:
            parts = [parts[i] + parts[i + 1] for i in range(0, len(parts), 2)]
        return parts[0]

    def in_plane(other):
        return z * PLANE + other

    def across(other):
        return other * PLANE + c

    gram1[c] = gram[...]
    sent1 = exchange(PLANE, c, gram, gram1, g1_send, g1_recv, in_plane)

    to_partner.wait()
    par_next = block(5, partner, y_next + hi)
    par_prev = block(6, partner, y_prev + hi)
    par_next.start()
    par_prev.start()

    plane_total = collect(PLANE, c, gram, gram1, g1_send, g1_recv, in_plane)
    gram_plane[...] = plane_total
    gram2[z] = plane_total
    sent2 = exchange(PLANES, z, gram_plane, gram2, g2_send, g2_recv, across)

    total = mine[...]
    for k in range(1, PLANES):
        other = (z + k) % PLANES
        remote(mine, plane_got.at[other], zl_send.at[k], zl_recv.at[other], tile=other * PLANE + c).wait_recv()
        total = total + plane_got[other]
    block_rows[...] = total
    for r in range(3):
        records[:, 100 * r:100 * r + 100] = block_rows[r, pl.ds(2 * z, 2), 0:100]

    par_next.wait()
    par_prev.wait()
    last_next = block(7, y_prev + 1 - hi, y_next + hi, 0)
    last_prev = block(8, y_next + 1 - hi, y_prev + hi, 1)
    last_next.start()
    last_prev.start()

    packed = collect(PLANES, z, gram_plane, gram2, g2_send, g2_recv, across)

    lane16 = lax.broadcasted_iota(jnp.int32, (16, 128), 1)
    row16 = lax.broadcasted_iota(jnp.int32, (16, 128), 0)
    system = jnp.concatenate([packed, pltpu.roll(packed, 96, 1)], 0)
    system = jnp.where(lane16 < 32, system, 0.0) + jnp.where(row16 == lane16, 15.0, 0.0)
    for p in range(16):
        pivot = system[p:p + 1, :] / system[p:p + 1, p:p + 1]
        system = jnp.where(row16 == p, pivot, system - system[:, p:p + 1] * pivot)
    combine = system - jnp.sum(system, axis=0, keepdims=True) * (1.0 / 16.0)
    combine = combine + jnp.where(row16 == lane16 - 16, 1.0, 0.0)
    for m in range(2):
        column = jnp.sum(jnp.where(lane16 == 16 + 8 * m + a, combine, 0.0), axis=1, keepdims=True)
        coef[m] = jnp.broadcast_to(column, (16, 128))

    on_next.wait()
    on_prev.wait()
    last_next.wait()
    last_prev.wait()

    factors = [[jnp.broadcast_to(coef[m, k:k + 1, :], (8, 128)) for k in range(16)] for m in range(2)]
    for r in range(0, 32, 8):
        for i in range(4):
            columns = slice(i * 128, (i + 1) * 128)
            sums = [None, None]
            for k in range(16):
                value = every[k // 2, k % 2, r:r + 8, columns]
                for m in range(2):
                    term = value * factors[m][8 * (k % 2) + k // 2]
                    sums[m] = term if sums[m] is None else sums[m] + term
            for m in range(2):
                updated[m, r:r + 8, columns] = sums[m]

    for copy in noise_copies + copies1 + copies2 + copies_z + sent1 + sent2:
        copy.wait_send()


def shards(surface, depth, land, gauge_cells, sigma, observed, noise):
    f32 = jnp.float32
    groups = jnp.pad(sigma.reshape(4, 100), ((0, 0), (0, 28)), constant_values=1.0)
    hbm = pl.BlockSpec(memory_space=pl.ANY)
    vmem = pl.BlockSpec(memory_space=pltpu.VMEM)
    dma = pltpu.SemaphoreType.DMA
    buffers = [
        (32, 512), None, None, (4, 128), (75, 128), (2, 9600), None, None,
        (ROWS, 8, 128), (ROWS * 4, 128), (ROWS, 8, 128), (ROWS, 8, 128), (ROWS, 8, 128), (ROWS, 8, 128),
        (6 * (OWN + 1) * 32, 128),
        (MEMBER_DEV, 2, 32, 512),
        (24, 8, 128), (PLANE, 3, 8, 128), (3, 8, 128), (MEMBER_DEV * 24, 128),
        (3, 8, 128), (MEMBER_DEV, 3, 8, 128), (3, 8, 128),
        (PLANES, 3, 8, 128), (3, 8, 128),
        (8, 128), (PLANE, 8, 128), (8, 128), (PLANES, 8, 128), (2, 16, 128),
    ]
    scratch = [pltpu.VMEM(shape, f32) if shape else None for shape in buffers]
    scratch[1] = pltpu.VMEM((32, 512), jnp.int32)
    for number in (2, 6, 7):
        scratch[number] = pltpu.SMEM((400,), jnp.int32)
    counts = (15, 4, 4, 8, 8, 8, 8, 8, 8, 4, 4, 8, 8, 4, 4, 9, 9)
    return pl.pallas_call(
        kernel,
        out_shape=(jax.ShapeDtypeStruct((2, 32, 512), f32), jax.ShapeDtypeStruct((2, 300), f32)),
        in_specs=[hbm] * 7,
        out_specs=(vmem, vmem),
        scratch_shapes=scratch + [dma((count,)) for count in counts],
        compiler_params=pltpu.CompilerParams(collective_id=0, has_side_effects=True),
    )(surface, depth, land, gauge_cells, groups, observed.reshape(75, 128), noise)


def solution(mesh):
    in_specs = (
        P("member", "tile", None),
        P("tile", None),
        P("tile", None),
        P(),
        P(),
        P(),
        P("member", None),
    )
    out_specs = (P("member", "tile", None), P("member", "tile"))
    return jax.shard_map(shards, mesh=mesh, in_specs=in_specs, out_specs=out_specs, check_vma=False)
```

time: 67.2 us -> 54.2 us (0.81)
  Pallas kernels: 61.4 us -> 49.9 us
  local copies, waits for them, and re-layouts: 4.92 us -> 3.5 us
    pallas_call x1, Pallas kernels: 61.4 us -> 49.9 us  [shards(): pl.pallas_call(kernel, out_shape=(jax.ShapeDtypeStruct((2, 32, 512), f32)...]
    reshape x1 -> x0, local copies, waits for them, and re-layouts: 1.42 us -> none  [shards(): observed.reshape(1, -1)]
where the time goes in v2:
time: 54.2 us; the launch traced here: 54 us
  Pallas kernels  49.9 us (92%)
  local copies, waits for them, and re-layouts  3.5 us (6%)
  between operations  0.65 us (1%)
    pallas_call x1, Pallas kernels, shards(): pl.pallas_call(kernel, out_shape=(jax.ShapeDtypeStruct((2, 32, 512), f32)...  49.9 us
    unnamed x4, local copies, waits for them, and re-layouts  2.15 us

profile of v2, /device:TPU:1, one launch (start us, length us, event | category | flops | bytes accessed | tf_op | source)
XLA Modules:
  0.0 54.0 jit_solution(8582577295853792267)
XLA Ops:
  0.6 0.8 %reshape.10 = f32[4,100]{1,0:T(4,128)S(1)} reshape(f32[400]{0:T(512)} %param.11) | data formatting | bytes 3200 | tf_op jit(solution)/shard_map/reshape | solution.py:404
  1.4 0.6 %pad.4.sigma_in = f32[4,128]{1,0:T(4,128)} pad(f32[4,100]{1,0:T(4,128)S(1)} %reshape.10, f32[]{:T(128)} %constant.0.clone.1), padding=0_0x0_28 | pad | bytes 3652 | tf_op jit(solution)/shard_map/jit(_pad)/pad | solution.py:404
  2.0 49.9 %shard_map.86 = (f32[2,32,512]{2,1,0:T(8,128)}, f32[2,300]{1,0:T(2,128)}) custom-call(f32[2,32,512]{2,1,0:T(8,128)} %surface.1, f32[32,512]{1,0:T(8,128)} %depth.1, s32[32,512]{1,0:T(8,128)} %land.1, s32[400]{0:T(512)} %cells_in.1, f32[4,128]{1,0:T(4,128)} %pad.4.sigma_in, f32[75,128]{1,0:T(8,128)} %bitcast.1, f32[2,9600]{1,0:T(2,128)} %noise_in.1), custom_call_target="tpu_custom_call" | custom-call | tf_op jit(solution)/shard_map/pallas_call | solution.py:423
  51.9 0.0 copy-start
  51.9 1.6 %copy.11 = f32[2,32,512]{2,1,0:T(8,128)} copy(f32[2,32,512]{2,1,0:T(8,128)} %get-tuple-element.4) | data formatting | bytes 262144
  53.5 0.0 copy-done
  53.5 0.6 %copy.12 = f32[2,300]{1,0:T(2,128)} copy(f32[2,300]{1,0:T(2,128)S(1)} %copy-done) | data formatting | bytes 4800
Async XLA Ops:
  51.9 1.6 %copy-start = (f32[2,300]{1,0:T(2,128)S(1)}, f32[2,300]{1,0:T(2,128)}, u32[]{:S(2)}) copy-start(f32[2,300]{1,0:T(2,128)} %get-tuple-element.5) | copy-start | bytes 7204

commit v3 on v2

--- a/solution.py
+++ b/solution.py
@@ -38,9 +38,9 @@
 
 def kernel(
     surface, depth, land, cells_in, sigma_in, observed_in, noise_in, updated, records,
-    depth_v, land_v, cells, sigma, observed, noise, starts, shifts,
+    depth_v, land_v, cells, sigma, observed, noise,
     lev, wet, frow, fcol, crow, ccol, hist, every, pieces, got1, mine, got2, own_noise, all_noise, obs,
-    plane_got, block_rows, gram, gram1, gram_plane, gram2, coef,
+    plane_got, block_rows, weight, gram, gram1, gram_plane, gram2, coef,
     local_sem, halo_send, halo_recv, noise_send, noise_recv, s1_send, s1_recv, s2_send, s2_recv,
     zl_send, zl_recv, g1_send, g1_recv, g2_send, g2_recv, sur_send, sur_recv,
 ):
@@ -133,7 +133,6 @@
     to_partner = block(0, a, partner)
     to_next = block(1, a, y_next + hi)
     to_prev = block(2, a, y_prev + hi)
-    to_partner.start()
     to_next.start()
     to_prev.start()
 
@@ -153,24 +152,11 @@
             )
             obs[r, p:p + 1, :] = merge(observed[pl.ds(first, 1), :], observed[pl.ds(after, 1), :], shift, lane1)
     all_noise[a] = own_noise[...]
-    noise_copies = []
-    for k in range(1, MEMBER_DEV):
-        noise_copies.append(
-            remote(own_noise, all_noise.at[a], noise_send.at[k], noise_recv.at[a], member=(a + k) % MEMBER_DEV)
-        )
-        noise_copies[-1].start()
-
-    table.wait()
-
-    def entry(j, carry):
-        for q in range(4):
-            cell = cells[q * 100 + j]
-            start = ((cell >> 9) & 31) * 32 + ((cell >> 7) & 3)
-            starts[q * 100 + j] = jnp.where((cell >> 14) == t, start, NO_GAUGE)
-            shifts[q * 100 + j] = (j - cell) & 127
-        return carry
-
-    lax.fori_loop(0, 100, entry, 0, unroll=5)
+    for q in range(4):
+        first, shift = 100 * q // 128, 100 * q % 128
+        after = min(first + 1, 3)
+        sig = merge(sigma[first:first + 1, :], sigma[after:after + 1, :], shift, lane1) if shift else sigma[0:1, :]
+        weight[q:q + 1, :] = jnp.where(lane1 < 100, 1.0 / (sig * sig), 0.0)
 
     edge = (lane == 127) & ((sub & 3) == 3)
 
@@ -193,6 +179,13 @@
     coefficients(HALO, HALO + OWN - 2)
     for copy in halos:
         copy.wait()
+    to_partner.start()
+    noise_copies = []
+    for k in range(1, MEMBER_DEV):
+        noise_copies.append(
+            remote(own_noise, all_noise.at[a], noise_send.at[k], noise_recv.at[a], member=(a + k) % MEMBER_DEV)
+        )
+        noise_copies[-1].start()
     coefficients(0, HALO)
     coefficients(HALO + OWN - 2, ROWS)
 
@@ -202,8 +195,8 @@
         flux = frow[low - 1:low] - crow[low - 1:low] * (lev[low:low + 1] - level)
         frow[low - 1:low] = flux
         group = (s % 6) * (OWN + 1)
-        for start in range(low, high, 8):
-            stop = min(start + 8, high)
+        for start in range(low, high, 16):
+            stop = min(start + 16, high)
             lane3 = lax.broadcasted_iota(jnp.int32, (stop - start, 8, 128), 2)
             level = lev[start:stop]
             rows_flux = frow[start:stop] - crow[start:stop] * (lev[start + 1:stop + 1] - level)
@@ -225,12 +218,23 @@
 
         lax.fori_loop(first, first + 8, one, 0)
 
+    to_next.wait()
+    to_prev.wait()
+    on_next = block(3, y_prev + hi, y_next + hi, 0)
+    on_prev = block(4, y_next + hi, y_prev + hi, 1)
+    on_next.start()
+    on_prev.start()
+
+    table.wait()
+
     def sample(j, totals):
         put = lane == j
         out = []
         for q in range(4):
-            start = starts[q * 100 + j]
-            shift = shifts[q * 100 + j]
+            cell = cells[q * 100 + j]
+            start = ((cell >> 9) & 31) * 32 + ((cell >> 7) & 3)
+            start = jnp.where((cell >> 14) == t, start, NO_GAUGE)
+            shift = (j - cell) & 127
             for s in range(6):
                 found = hist[pl.ds(s * (OWN + 1) * 32 + start, 8, stride=4), :]
                 out.append(jnp.where(put, pltpu.roll(found, shift, 1), totals[q * 6 + s]))
@@ -274,12 +278,11 @@
         copies_z.append(remote(mine, plane_got.at[z], zl_send.at[k], zl_recv.at[z], tile=other * PLANE + c))
         copies_z[-1].start()
 
-    to_next.wait()
-    to_prev.wait()
-    on_next = block(3, y_prev + hi, y_next + hi, 0)
-    on_prev = block(4, y_next + hi, y_prev + hi, 1)
-    on_next.start()
-    on_prev.start()
+    to_partner.wait()
+    par_next = block(5, partner, y_next + hi)
+    par_prev = block(6, partner, y_prev + hi)
+    par_next.start()
+    par_prev.start()
 
     for k in range(1, MEMBER_DEV):
         other = (a + k) % MEMBER_DEV
@@ -292,8 +295,7 @@
     for p in range(PLANES):
         for r in range(3):
             group = ((p * PLANE + c) * 3 + r) % 4
-            sig = sigma[pl.ds(group, 1), :]
-            wgt = jnp.where(lane1 < 100, 1.0 / (sig * sig), 0.0)
+            wgt = weight[pl.ds(group, 1), :]
             rec = jnp.concatenate(
                 [got2[pl.ds(8 * r + 2 * p + m, 8, stride=24), :] for m in range(2)], 0
             )
@@ -335,11 +337,12 @@
     gram1[c] = gram[...]
     sent1 = exchange(PLANE, c, gram, gram1, g1_send, g1_recv, in_plane)
 
-    to_partner.wait()
-    par_next = block(5, partner, y_next + hi)
-    par_prev = block(6, partner, y_prev + hi)
-    par_next.start()
-    par_prev.start()
+    par_next.wait()
+    par_prev.wait()
+    last_next = block(7, y_prev + 1 - hi, y_next + hi, 0)
+    last_prev = block(8, y_next + 1 - hi, y_prev + hi, 1)
+    last_next.start()
+    last_prev.start()
 
     plane_total = collect(PLANE, c, gram, gram1, g1_send, g1_recv, in_plane)
     gram_plane[...] = plane_total
@@ -354,13 +357,6 @@
     block_rows[...] = total
     for r in range(3):
         records[:, 100 * r:100 * r + 100] = block_rows[r, pl.ds(2 * z, 2), 0:100]
-
-    par_next.wait()
-    par_prev.wait()
-    last_next = block(7, y_prev + 1 - hi, y_next + hi, 0)
-    last_prev = block(8, y_next + 1 - hi, y_prev + hi, 1)
-    last_next.start()
-    last_prev.start()
 
     packed = collect(PLANES, z, gram_plane, gram2, g2_send, g2_recv, across)
 
@@ -401,24 +397,23 @@
 
 def shards(surface, depth, land, gauge_cells, sigma, observed, noise):
     f32 = jnp.float32
-    groups = jnp.pad(sigma.reshape(4, 100), ((0, 0), (0, 28)), constant_values=1.0)
+    groups = jnp.pad(sigma, (0, 112), constant_values=1.0).reshape(4, 128)
     hbm = pl.BlockSpec(memory_space=pl.ANY)
     vmem = pl.BlockSpec(memory_space=pltpu.VMEM)
     dma = pltpu.SemaphoreType.DMA
     buffers = [
-        (32, 512), None, None, (4, 128), (75, 128), (2, 9600), None, None,
+        (32, 512), None, None, (4, 128), (75, 128), (2, 9600),
         (ROWS, 8, 128), (ROWS * 4, 128), (ROWS, 8, 128), (ROWS, 8, 128), (ROWS, 8, 128), (ROWS, 8, 128),
         (6 * (OWN + 1) * 32, 128),
         (MEMBER_DEV, 2, 32, 512),
         (24, 8, 128), (PLANE, 3, 8, 128), (3, 8, 128), (MEMBER_DEV * 24, 128),
         (3, 8, 128), (MEMBER_DEV, 3, 8, 128), (3, 8, 128),
-        (PLANES, 3, 8, 128), (3, 8, 128),
+        (PLANES, 3, 8, 128), (3, 8, 128), (8, 128),
         (8, 128), (PLANE, 8, 128), (8, 128), (PLANES, 8, 128), (2, 16, 128),
     ]
     scratch = [pltpu.VMEM(shape, f32) if shape else None for shape in buffers]
     scratch[1] = pltpu.VMEM((32, 512), jnp.int32)
-    for number in (2, 6, 7):
-        scratch[number] = pltpu.SMEM((400,), jnp.int32)
+    scratch[2] = pltpu.SMEM((400,), jnp.int32)
     counts = (15, 4, 4, 8, 8, 8, 8, 8, 8, 4, 4, 8, 8, 4, 4, 9, 9)
     return pl.pallas_call(
         kernel,

time: 54.2 us -> 49.3 us (0.910)
  Pallas kernels: 49.9 us -> 45.1 us
    pallas_call x1, Pallas kernels: 49.9 us -> 45.1 us  [shards(): pl.pallas_call(kernel, out_shape=(jax.ShapeDtypeStruct((2, 32, 512), f32)...]
    pad x1 -> x0, local copies, waits for them, and re-layouts: 0.59 us -> none  [shards(): jnp.pad(sigma.reshape(4, 100), ((0, 0), (0, 28)), constant_values=1.0)]
where the time goes in v3:
time: 49.3 us; the launch traced here: 49.2 us
  Pallas kernels  45.1 us (91%)
  local copies, waits for them, and re-layouts  3.41 us (7%)
  between operations  0.65 us (1%)
    pallas_call x1, Pallas kernels, shards(): pl.pallas_call(kernel, out_shape=(jax.ShapeDtypeStruct((2, 32, 512), f32)...  45.1 us
    unnamed x4, local copies, waits for them, and re-layouts  2.15 us
    reshape x1, local copies, waits for them, and re-layouts, shards(): groups = jnp.pad(sigma, (0, 112), constant_values=1.0).reshape(4, 128)  1.26 us

profile of v3, /device:TPU:1, one launch (start us, length us, event | category | flops | bytes accessed | tf_op | source)
XLA Modules:
  0.0 49.2 jit_solution(1723270225820536249)
XLA Ops:
  0.6 1.3 %pad_bitcast_fusion.sigma_in = f32[4,128]{1,0:T(4,128)} fusion(f32[400]{0:T(512)} %param.11), kind=kLoop, calls=%fused_computation | loop fusion | bytes 3648 | tf_op jit(solution)/shard_map/reshape | solution.py:400
  1.9 45.1 %shard_map.86 = (f32[2,32,512]{2,1,0:T(8,128)}, f32[2,300]{1,0:T(2,128)}) custom-call(f32[2,32,512]{2,1,0:T(8,128)} %surface.1, f32[32,512]{1,0:T(8,128)} %depth.1, s32[32,512]{1,0:T(8,128)} %land.1, s32[400]{0:T(512)} %cells_in.1, f32[4,128]{1,0:T(4,128)} %pad_bitcast_fusion.sigma_in, f32[75,128]{1,0:T(8,128)} %bitcast.3, f32[2,9600]{1,0:T(2,128)} %noise_in.1), custom_call_target="tpu_custom_call" | custom-call | tf_op jit(solution)/shard_map/pallas_call | solution.py:418
  47.0 0.0 copy-start
  47.0 1.6 %copy.11 = f32[2,32,512]{2,1,0:T(8,128)} copy(f32[2,32,512]{2,1,0:T(8,128)} %get-tuple-element.4) | data formatting | bytes 262144
  48.6 0.0 copy-done
  48.6 0.6 %copy.12 = f32[2,300]{1,0:T(2,128)} copy(f32[2,300]{1,0:T(2,128)S(1)} %copy-done) | data formatting | bytes 4800
Async XLA Ops:
  47.0 1.6 %copy-start = (f32[2,300]{1,0:T(2,128)S(1)}, f32[2,300]{1,0:T(2,128)}, u32[]{:S(2)}) copy-start(f32[2,300]{1,0:T(2,128)} %get-tuple-element.5) | copy-start | bytes 7204
